TPU v7x, 128 devices: a whole 4x4x4 slice. The times are simulated.
128 devices in a mesh: row: 32 (over y, z_lo, x), col: 4 (over z_hi, core).
Axes of the slice: x: 4, y: 4, z: 4 (z_hi: 2, z_lo: 2; z = z_hi * 2 + z_lo), core: 2. Of those that a mesh axis runs over, the one named last changes fastest.
Arguments:
- samples: float32 [131072, 32], P(('row', 'col')), may hold values from -3 to 3
- sample_logw: float32 [131072], P(('row', 'col')), may hold values from -8 to 8
- references: float32 [65536, 32], P(('row', 'col')), may hold values from -3 to 3
- reference_logw: float32 [65536], P(('row', 'col')), may hold values from -8 to 8
- dual_start: float32 [32, 4096], P('row'), may hold values from -3 to 3
- kept_tiles: int32 [32, 4, 32], P('row', 'col'), may hold values from 0 to 255, as said below
- tile_counts: int32 [32, 4], P('row', 'col'), may hold values from 2 to 32, as said below
Outputs:
- row_duals: float32 [32, 4096], P('row')
- col_duals: float32 [4, 16384], P('col')
Inputs may be any that keep to these rules, and one draw needn't show every extreme that they name: `kept_tiles`: on device (i, j) the first tile_counts[i, j] entries are distinct tiles r * 32 + c of its 8 by 32 grid; later entries are tiles of that grid and unused. Every block of every sample group and of every reference group lies in some used tile. `tile_counts`: 32 on at least one device.
All inputs are finite; a program needn't handle non-finite values.
Results may differ from a plain program's by a relative error of at most 0.0003.
Values sent between devices are 32-bit elements; how exact they have to be, the bound alone decides.
A program may use at most 64 MiB of HBM per device.

v0:
```python
import jax
import jax.numpy as jnp
from jax import lax
from jax.sharding import Mesh
from jax.sharding import PartitionSpec as P

TILE = 512
ITERS = 3
ROW = ("row_0", "row_1", "row_2")
ROW_COL = ("row_0", "row_1", "row_2", "col")


lowest = -1e30
epsilon = 0.1


def side_by_side(arrays, axis, dim, along):
    columns = [a.reshape(*a.shape[:along], -1) for a in arrays]
    both = jnp.concatenate(columns, axis=along)
    whole, at, gathered = (lax.all_gather(both, axis, axis=dim, tiled=True), 0, [])
    for a, column in zip(arrays, columns):
        piece = whole[..., at : at + column.shape[along]]
        gathered.append(piece.reshape(*piece.shape[:along], *a.shape[along:]))
        at += column.shape[along]
    return tuple(gathered)


def from_partner(shard, axis, distance):
    return lax.ppermute(shard, axis, [(i, i ^ 1 << distance) for i in range(lax.axis_size(axis))])


def combined_by_axis(shard, axes, combine):
    for axis in axes:
        pieces = jax.tree.map(lambda part: lax.all_gather(part, axis), shard)
        shard = jax.tree.map(lambda part: part[0], pieces)
        for k in range(1, lax.axis_size(axis)):
            shard = combine(shard, jax.tree.map(lambda part: part[k], pieces))
    return shard


def from_everyone(shard, axis):
    devices = lax.axis_size(axis)
    return lax.all_to_all(
        jnp.broadcast_to(shard[None], (devices, *shard.shape)), axis, 0, 0, tiled=True
    )


def all_in_one(shard, axis):
    leaves = jax.tree.leaves(shard)
    turns = sorted(range(len(leaves)), key=lambda k: -leaves[k].size)
    width = (1, *leaves[turns[0]].shape)[-1]
    lines = [
        jnp.pad(leaves[k].reshape(-1), (0, -leaves[k].size % width)).reshape(-1, width)
        for k in turns
    ]
    both, at, found = (from_everyone(jnp.concatenate(lines), axis), 0, {})
    for k, line in zip(turns, lines):
        piece = both[:, at : at + len(line)].reshape(len(both), -1)
        found[k] = piece[:, : leaves[k].size].reshape(-1, *leaves[k].shape)
        at += len(line)
    numbers = iter(range(len(leaves)))
    return jax.tree.map(lambda _: found[next(numbers)], shard)


def folded_in_pairs(pieces, combine):
    while len(jax.tree.leaves(pieces)[0]) > 1:
        pieces = jax.vmap(combine)(
            *(jax.tree.map(lambda part: part[side::2], pieces) for side in (0, 1))
        )
    return jax.tree.map(lambda part: part[0], pieces)


def joined_all(shard, axis, combine):
    pieces = all_in_one(shard, axis)
    return folded_in_pairs(pieces, combine)


def combine(left, right):
    peak = jnp.maximum(left[0], right[0])
    return (peak, left[1] * jnp.exp(left[0] - peak) + right[1] * jnp.exp(right[0] - peak))


def tile_cost(row_points, row_norms, col_points, col_norms):
    inner = jnp.dot(
        row_points,
        col_points.T,
        precision=lax.Precision.HIGHEST,
        preferred_element_type=jnp.float32,
    )
    return row_norms[:, None] + col_norms[None, :] - 2.0 * inner


def per_device(
    samples, sample_logw, references, reference_logw, dual_start, kept_tiles, tile_counts
):
    sample_group, sample_weights = side_by_side((samples, sample_logw), "col", 0, 1)
    reference_group, reference_weights = side_by_side((references, reference_logw), ROW, 0, 1)
    block = TILE
    slots = kept_tiles.shape[2]
    col_blocks = reference_group.shape[0] // block
    sample_norms = jnp.sum(sample_group * sample_group, axis=1)
    reference_norms = jnp.sum(reference_group * reference_group, axis=1)
    own_tiles = kept_tiles[0, 0]
    own_count = tile_counts[0]
    partner_group, partner_weights, partner_tiles, partner_count = from_partner(
        (sample_group, sample_weights, own_tiles, own_count), ROW, 0
    )
    is_low = lax.axis_index(ROW) % 2 == 0
    low_tiles = jnp.where(is_low, own_tiles, partner_tiles)
    high_tiles = jnp.where(is_low, partner_tiles, own_tiles)
    low_count = jnp.where(is_low, own_count[0], partner_count[0])
    high_count = jnp.where(is_low, partner_count[0], own_count[0])
    half = (low_count + high_count + 1) // 2
    first = jnp.where(is_low, 0, half)
    work = jnp.where(is_low, half, low_count + high_count - half)

    def locate(step):
        position = first + step
        from_low = position < low_count
        tile = jnp.where(
            from_low,
            low_tiles[jnp.minimum(position, slots - 1)],
            high_tiles[jnp.clip(position - low_count, 0, slots - 1)],
        )
        source = jnp.where(from_low == is_low, 0, 1).astype(jnp.int32)
        return (source, tile)

    group_stack = jnp.stack([sample_group, partner_group])
    weight_stack = jnp.stack([sample_weights, partner_weights])
    norm_stack = jnp.stack([sample_norms, jnp.sum(partner_group * partner_group, axis=1)])
    sources = group_stack.shape[0]
    row_width = group_stack.shape[1]
    col_width = reference_group.shape[0]

    def cost_at(step):
        source, tile = locate(step)
        row_start = tile // col_blocks * block
        col_start = tile % col_blocks * block
        row_points = lax.dynamic_slice(
            group_stack, (source, row_start, 0), (1, block, group_stack.shape[2])
        )[0]
        row_norms = lax.dynamic_slice(norm_stack, (source, row_start), (1, block))[0]
        col_points = lax.dynamic_slice_in_dim(reference_group, col_start, block, 0)
        col_norms = lax.dynamic_slice_in_dim(reference_norms, col_start, block, 0)
        return (
            source,
            row_start,
            col_start,
            tile_cost(row_points, row_norms, col_points, col_norms),
        )

    dual_row = dual_start[0]
    dual_col = jnp.zeros((col_width,), jnp.float32)
    for turn in range(ITERS):
        dual_stack = jnp.stack([dual_row, from_partner(dual_row, ROW, 0)])

        def column_visit(step, carry):
            source, row_start, col_start, cost = cost_at(step)
            weights = lax.dynamic_slice(weight_stack, (source, row_start), (1, block))[0]
            duals = lax.dynamic_slice(dual_stack, (source, row_start), (1, block))[0]
            score = weights[:, None] + (duals[:, None] - cost) / epsilon
            peak = jnp.max(score, axis=0)
            total = jnp.sum(jnp.exp(score - peak[None, :]), axis=0)
            before = (
                lax.dynamic_slice_in_dim(carry[0], col_start, block, 0),
                lax.dynamic_slice_in_dim(carry[1], col_start, block, 0),
            )
            merged = combine(before, (peak, total))
            return (
                lax.dynamic_update_slice_in_dim(carry[0], merged[0], col_start, 0),
                lax.dynamic_update_slice_in_dim(carry[1], merged[1], col_start, 0),
            )

        column_start_state = (
            jnp.full((col_width,), lowest, jnp.float32),
            jnp.zeros((col_width,), jnp.float32),
        )
        col_peak, col_total = combined_by_axis(
            lax.fori_loop(0, work, column_visit, column_start_state), ROW, combine
        )
        dual_col = -epsilon * (col_peak + jnp.log(col_total))

        def row_visit(step, carry):
            source, row_start, col_start, cost = cost_at(step)
            weights = lax.dynamic_slice_in_dim(reference_weights, col_start, block, 0)
            duals = lax.dynamic_slice_in_dim(dual_col, col_start, block, 0)
            score = weights[None, :] + (duals[None, :] - cost) / epsilon
            peak = jnp.max(score, axis=1)
            total = jnp.sum(jnp.exp(score - peak[:, None]), axis=1)
            before = (
                lax.dynamic_slice(carry[0], (source, row_start), (1, block))[0],
                lax.dynamic_slice(carry[1], (source, row_start), (1, block))[0],
            )
            merged = combine(before, (peak, total))
            return (
                lax.dynamic_update_slice(carry[0], merged[0][None], (source, row_start)),
                lax.dynamic_update_slice(carry[1], merged[1][None], (source, row_start)),
            )

        start_state = (
            jnp.full((sources, row_width), lowest, jnp.float32),
            jnp.zeros((sources, row_width), jnp.float32),
        )
        row_peaks, row_sums = lax.fori_loop(0, work, row_visit, start_state)
        returned = from_partner((row_peaks[1], row_sums[1]), ROW, 0)
        row_peak, row_total = joined_all(
            combine((row_peaks[0], row_sums[0]), returned), "col", combine
        )
        dual_row = -epsilon * (row_peak + jnp.log(row_total))
    return (dual_row[None], dual_col[None])


def solution(mesh):
    finer = Mesh(
        mesh.devices.reshape(4, 2, 4, mesh.shape["col"]), ("row_0", "row_1", "row_2", "col")
    )
    in_specs = (
        P(ROW_COL, None),
        P(ROW_COL),
        P(ROW_COL, None),
        P(ROW_COL),
        P(ROW, None),
        P(ROW, "col", None),
        P(ROW, "col"),
    )
    out_specs = (P(ROW, None), P("col", None))
    return jax.shard_map(
        per_device, mesh=finer, in_specs=in_specs, out_specs=out_specs, check_vma=False
    )
```

profile of v0, /device:TPU:1, one launch (start us, length us, event | category | flops | bytes accessed | tf_op | source)
XLA Modules:
  0.0 975.5 jit_solution(17208234660353493933)
XLA Ops:
  13.2 11.6 %all_gather.91 = f32[4096,33]{0,1:T(8,128)S(1)} all-gather(f32[1024,33]{0,1:T(8,128)S(1)} %pad_maximum_fusion.1), channel_id=1, replica_groups=mesh['row_0'=4,'row_1'=2,'row_2'=4,'col'=4] {'col'}, dimensions={0}, use_global_device_ids=true | all-gather | bytes 675840 | tf_op jit(solution)/shard_map/all_gather | solution.py:20
  30.0 10.8 %collective-permute-done.4 = f32[4096,32]{0,1:T(8,128)S(1)} collective-permute-done((f32[4096,32]{0,1:T(8,128)S(1)}, f32[4096,32]{0,1:T(8,128)S(1)}, u32[]{:S(2)}, u32[]{:S(2)}) %collective-permute-start.4) | collective-permute-done | bytes 524320 | tf_op jit(solution)/shard_map/ppermute | solution.py:29
  43.7 101.2 %all-gather.20.cloned.1.call-done = f32[16384,33]{0,1:T(8,128)} async-done(((f32[512,33]{0,1:T(8,128)}), f32[16384,33]{0,1:T(8,128)}) %all-gather.20.cloned.1.call-update) | async-done | bytes 2162704 | tf_op jit(solution)/shard_map/all_gather | solution.py:20
  151.6 93.5 %while.84 = (s32[]{:T(128)}, f32[16384]{0:T(1024)S(1)}, f32[16384]{0:T(1024)S(1)}, s32[]{:T(128)}, s32[]{:T(128)}, /*index=5*/s32[]{:T(128)}, s32[32]{0:T(128)S(...) while((s32[]{:T(128)}, f32[16384]{0:T(1024)S(1)}, ...), condition=%wide.region_6.7_spmd, body=%wide.region_3.6_spmd.sunk | while | flops 103024680 | bytes 2665136 | solution.py:179
  245.1 9.5 all-gather.1
  254.6 9.4 all-gather
  272.4 9.4 all-gather.7
  281.8 9.4 all-gather.9
  291.3 98.8 %while.85 = (s32[]{:T(128)}, f32[2,4096]{1,0:T(2,128)S(1)}, f32[2,4096]{1,0:T(2,128)S(1)}, s32[]{:T(128)}, s32[]{:T(128)}, /*index=5*/s32[]{:T(128)}, pred[]{:T(...) while((s32[]{:T(128)}, f32[2,4096]{1,0:T(2,128)S(1)}, ...), condition=%wide.region_10.11_spmd, body=%wide.region_7.10_spmd.sunk | while | flops 103024680 | bytes 2673340 | solution.py:204
  393.2 32.6 %all_to_all.15 = f32[4,2,4096]{2,1,0:T(2,128)S(1)} all-to-all(f32[4,2,4096]{2,1,0:T(2,128)S(1)} %broadcast_in_dim.8), channel_id=1, replica_groups=mesh['row_0'=4,'row_1'=2,'row_2'=4,'col'=4] {'col'}, dimensions={0} | all-to-all | bytes 262144 | tf_op jit(solution)/shard_map/all_to_all | solution.py:43
  429.5 92.9 %while.86 = (s32[]{:T(128)}, f32[16384]{0:T(1024)S(1)}, f32[16384]{0:T(1024)S(1)}, s32[]{:T(128)}, s32[]{:T(128)}, /*index=5*/s32[]{:T(128)}, s32[32]{0:T(128)S(...) while((s32[]{:T(128)}, f32[16384]{0:T(1024)S(1)}, ...), condition=%wide.region_14.15_spmd, body=%wide.region_11.14_spmd.sunk | while | flops 103024680 | bytes 2665136 | solution.py:179
  522.4 16.5 %all-gather.3 = f32[65536]{0:T(1024)S(1)} all-gather(f32[16384]{0:T(1024)S(1)} %get-tuple-element.1159), channel_id=5, replica_groups=mesh['row_0'=4,'row_1'=2,'row_2'=4,'col'=4] {'row_0'}, dimensions={0}, use_global_device_ids=true | all-gather | bytes 327680 | tf_op jit(solution)/shard_map/all_gather | solution.py:34
  538.9 10.2 %all-gather.2 = f32[65536]{0:T(1024)S(1)} all-gather(f32[16384]{0:T(1024)S(1)} %get-tuple-element.1158), channel_id=4, replica_groups=mesh['row_0'=4,'row_1'=2,'row_2'=4,'col'=4] {'row_0'}, dimensions={0}, use_global_device_ids=true | all-gather | bytes 327680 | tf_op jit(solution)/shard_map/all_gather | solution.py:34
  560.7 11.4 %all-gather.11 = f32[4,1,16384]{2,1,0:T(1,128)S(1)} all-gather(f32[1,1,16384]{2,1,0:T(1,128)S(1)} %get-tuple-element.1539), channel_id=1, replica_groups=mesh['row_0'=4,'row_1'=2,'row_2'=4,'col'=4] {'row_2'}, dimensions={0}, use_global_device_ids=true | all-gather | bytes 327680 | tf_op jit(solution)/shard_map/all_gather | solution.py:34
  572.1 9.4 all-gather.13
  581.7 99.3 %while.87 = (s32[]{:T(128)}, f32[2,4096]{1,0:T(2,128)S(1)}, f32[2,4096]{1,0:T(2,128)S(1)}, s32[]{:T(128)}, s32[]{:T(128)}, /*index=5*/s32[]{:T(128)}, pred[]{:T(...) while((s32[]{:T(128)}, f32[2,4096]{1,0:T(2,128)S(1)}, ...), condition=%wide.region_18.19_spmd, body=%wide.region_15.18_spmd.sunk | while | flops 103024680 | bytes 2673340 | solution.py:204
  683.9 12.4 %all_to_all.16 = f32[4,2,4096]{2,1,0:T(2,128)S(1)} all-to-all(f32[4,2,4096]{2,1,0:T(2,128)S(1)} %broadcast_in_dim.9), channel_id=1, replica_groups=mesh['row_0'=4,'row_1'=2,'row_2'=4,'col'=4] {'col'}, dimensions={0} | all-to-all | bytes 262144 | tf_op jit(solution)/shard_map/all_to_all | solution.py:43
  700.1 92.7 %while.88 = (s32[]{:T(128)}, f32[16384]{0:T(1024)S(1)}, f32[16384]{0:T(1024)S(1)}, s32[]{:T(128)}, s32[]{:T(128)}, /*index=5*/s32[]{:T(128)}, s32[32]{0:T(128)S(...) while((s32[]{:T(128)}, f32[16384]{0:T(1024)S(1)}, ...), condition=%wide.region_22.23_spmd, body=%wide.region_19.22_spmd.sunk | while | flops 103024680 | bytes 2665136 | solution.py:179
  792.8 14.4 %all-gather.5 = f32[65536]{0:T(1024)S(1)} all-gather(f32[16384]{0:T(1024)S(1)} %get-tuple-element.1163), channel_id=7, replica_groups=mesh['row_0'=4,'row_1'=2,'row_2'=4,'col'=4] {'row_0'}, dimensions={0}, use_global_device_ids=true | all-gather | bytes 327680 | tf_op jit(solution)/shard_map/all_gather | solution.py:34
  807.3 10.2 %all-gather.4 = f32[65536]{0:T(1024)S(1)} all-gather(f32[16384]{0:T(1024)S(1)} %get-tuple-element.1162), channel_id=6, replica_groups=mesh['row_0'=4,'row_1'=2,'row_2'=4,'col'=4] {'row_0'}, dimensions={0}, use_global_device_ids=true | all-gather | bytes 327680 | tf_op jit(solution)/shard_map/all_gather | solution.py:34
  818.0 9.0 all-gather.14
  830.9 10.1 %all-gather.15 = f32[4,1,16384]{2,1,0:T(1,128)S(1)} all-gather(f32[1,1,16384]{2,1,0:T(1,128)S(1)} %get-tuple-element.1535), channel_id=1, replica_groups=mesh['row_0'=4,'row_1'=2,'row_2'=4,'col'=4] {'row_2'}, dimensions={0}, use_global_device_ids=true | all-gather | bytes 327680 | tf_op jit(solution)/shard_map/all_gather | solution.py:34
  841.0 10.0 %all-gather.17 = f32[4,1,16384]{2,1,0:T(1,128)S(1)} all-gather(f32[1,1,16384]{2,1,0:T(1,128)S(1)} %get-tuple-element.1536), channel_id=1, replica_groups=mesh['row_0'=4,'row_1'=2,'row_2'=4,'col'=4] {'row_2'}, dimensions={0}, use_global_device_ids=true | all-gather | bytes 327680 | tf_op jit(solution)/shard_map/all_gather | solution.py:34
  851.2 99.6 %while.89 = (s32[]{:T(128)}, f32[2,4096]{1,0:T(2,128)S(1)}, f32[2,4096]{1,0:T(2,128)S(1)}, s32[]{:T(128)}, s32[]{:T(128)}, /*index=5*/s32[]{:T(128)}, pred[]{:T(...) while((s32[]{:T(128)}, f32[2,4096]{1,0:T(2,128)S(1)}, ...), condition=%wide.region_26.27_spmd, body=%wide.region_23.26_spmd.sunk | while | flops 103024680 | bytes 2673340 | solution.py:204
  (1146 shorter events, 518.1 us)
Async XLA Ops:
  7.2 137.7 %all-gather.20.cloned.1.call-start = ((), (), s32[]{:S(2)}) async-start(), calls=%async_computation.3 | async-start | bytes 2703360 | tf_op jit(solution)/shard_map/all_gather | solution.py:20
  8.7 19.8 %collective-permute-start.1 = (s32[32]{0:T(128)}, s32[32]{0:T(128)S(1)}, u32[]{:S(2)}, u32[]{:S(2)}) collective-permute-start(s32[32]{0:T(128)} %bitcast.551), channel_id=1, source_target_pairs={{0,4},{4,0},{8,12},{12,8},{16,20},{20,16},{24,28},{28,24},{32,36},... | collective-permute-start | bytes 392 | tf_op jit(solution)/shard_map/ppermute | solution.py:29
  10.8 16.4 %collective-permute-start = (s32[1]{0:T(128)}, s32[1]{0:T(128)}, u32[]{:S(2)}, u32[]{:S(2)}) collective-permute-start(s32[1]{0:T(128)} %bitcast.37), channel_id=1, source_target_pairs={{0,4},{4,0},{8,12},{12,8},{16,20},{20,16},{24,28},{28,24},{32,36},... | collective-permute-start | bytes 20 | tf_op jit(solution)/shard_map/ppermute | solution.py:29
  10.9 18.3 %collective-permute-start.3 = (f32[4096]{0:T(1024)}, f32[4096]{0:T(1024)S(1)}, u32[]{:S(2)}, u32[]{:S(2)}) collective-permute-start(f32[4096]{0:T(1024)} %bitcast.538), channel_id=1, source_target_pairs={{0,4},{4,0},{8,12},{12,8},{16,20},{20,16},{24,28},{28,24},{32,36},... | collective-permute-start | bytes 49160 | tf_op jit(solution)/shard_map/ppermute | solution.py:29
  24.9 5.1 collective-permute-start.2
  25.3 15.5 %collective-permute-start.4 = (f32[4096,32]{0,1:T(8,128)S(1)}, f32[4096,32]{0,1:T(8,128)S(1)}, u32[]{:S(2)}, u32[]{:S(2)}) collective-permute-start(f32[4096,32]{0,1:T(8,128)S(1)} %get-tuple-element.1476), channel_id=1, source_target_pairs={{0,4},{4,0},{8,12},{12,8},{16,20},{20,16},{24,28},{28,24},{32,36},... | collective-permute-start | bytes 1572872 | tf_op jit(solution)/shard_map/ppermute | solution.py:29
  245.1 46.2 %slice-start = ((f32[16384,33]{0,1:T(8,128)}), f32[16384,1]{0,1:T(1,128)S(1)}, s32[]{:S(2)}) async-start(f32[16384,33]{0,1:T(8,128)} %all-gather.20.cloned.1.call-done), calls=%async_computation.4 | async-start | bytes 131072 | tf_op jit(solution)/shard_map/slice | solution.py:22
  390.3 2.7 collective-permute-start.5
  390.3 2.8 collective-permute-start.6
  426.7 2.8 collective-permute-start.7
  681.0 2.7 collective-permute-start.9
  681.1 2.7 collective-permute-start.8
  697.2 2.9 collective-permute-start.10
  950.8 2.7 collective-permute-start.12
  950.9 2.7 collective-permute-start.11
  954.4 12.8 %all-to-all-start.2 = ((f32[4,2,4096]{2,1,0:T(2,128)}), f32[4,2,4096]{2,1,0:T(2,128)S(1)}, u32[]{:S(2)}, u32[]{:S(2)}) async-start(f32[4,2,4096]{2,1,0:T(2,128)} %broadcast_in_dim.16), calls=%async_computation.2 | async-start | bytes 262144 | tf_op jit(solution)/shard_map/all_to_all | solution.py:43
Sparse Core Ops, SparseCore 0:
  9.6 135.2 all-gather.19
where the time goes:
time: 991 us; the launch traced here: 975 us
  matrix products  228 us (23%)
  blocking collectives  218 us (22%)
  local copies, waits for them, and re-layouts  190 us (19%)
  loops' own time  134 us (14%)
  waiting for transfers between devices  122 us (12%)
  other arithmetic  46.9 us (5%)
  starting transfers between devices  21.1 us (2%)
  between operations  16.5 us (2%)
    dot_general x102, matrix products, tile_cost(): jnp.dot(row_points, col_points.T, precision=lax.Precision.HIGHEST, prefer...  228 us
    all_gather x18, blocking collectives, combined_by_axis(): pieces = jax.tree.map(lambda part: lax.all_gather(part, axis), shard)  161 us
    all_gather x1, waiting for transfers between devices, side_by_side(): lax.all_gather(both, axis, axis=dim, tiled=True)  101 us
    another operation x3, loops' own time, per_device(): row_peaks, row_sums = lax.fori_loop(0, work, row_visit, start_state)  66.8 us
    another operation x3, loops' own time, per_device(): lax.fori_loop(0, work, column_visit, column_start_state)  66.7 us
    dynamic_slice x102, local copies, waits for them, and re-layouts, locate(): high_tiles[jnp.clip(position - low_count, 0, slots - 1)]  63 us
    dynamic_slice x102, local copies, waits for them, and re-layouts, locate(): low_tiles[jnp.minimum(position, slots - 1)]  59.1 us
    all_to_all x2, blocking collectives, from_everyone(): lax.all_to_all(jnp.broadcast_to(shard[None], (devices, *shard.shape)), ax...  45 us
  transfers between devices with their start and end apart: 15, of which 11 were waited for; matrix products, arithmetic and copies ran while one was open for 1% of the time, Pallas kernels for 0%

commit v1 on v0

v1 whole, which is shorter than its diff:
```python
import functools

import jax
import jax.numpy as jnp
from jax import lax
from jax.experimental import pallas as pl
from jax.experimental.pallas import tpu as pltpu
from jax.sharding import PartitionSpec as P

TILE = 512
ITERS = 3
LANES = 128
PIECES = TILE // LANES
DEPTH = 128
BIAS = 16
MESH = pl.DeviceIdType.MESH

lowest = -1e30
epsilon = 0.1
LOG2E = 1.4426950408889634
LN2 = 0.6931471805599453
SCALE = 2.0 / epsilon * LOG2E


def lse(values):
    peak = jnp.max(values, axis=0, keepdims=True)
    return peak + jnp.log2(jnp.sum(jnp.exp2(values - peak), axis=0, keepdims=True))


def halves(values):
    high = values.astype(jnp.bfloat16)
    low = (values - high.astype(jnp.float32)).astype(jnp.bfloat16)
    return high, low


def place_points(points, reduced, kept, slot):
    high, low = halves(points)
    dim = points.shape[0]
    top = BIAS + 3 * dim
    for ref, order in ((reduced, (high, high, low)), (kept, (high, low, high))):
        for k, part in enumerate(order):
            ref[slot, BIAS + k * dim : BIAS + (k + 1) * dim, :] = part
        ref[slot, top:, :] = jnp.zeros((DEPTH - top, TILE), jnp.bfloat16)
    kept[slot, :BIAS, :] = jnp.ones((BIAS, TILE), jnp.bfloat16)


def place_bias(rows, reduced, slot):
    index = lax.broadcasted_iota(jnp.int32, (BIAS, LANES), 0)
    for piece in range(PIECES):
        row = rows[piece : piece + 1, :]
        first = row.astype(jnp.bfloat16).astype(jnp.float32)
        rest = row - first
        second = rest.astype(jnp.bfloat16).astype(jnp.float32)
        third = rest - second
        tile = jnp.where(
            index == 0,
            first,
            jnp.where(index == 1, second, jnp.where(index == 2, third, 0.0)),
        )
        reduced[slot, :BIAS, piece * LANES : (piece + 1) * LANES] = tile.astype(jnp.bfloat16)


def cut(line):
    return [line[:, k * LANES : (k + 1) * LANES] for k in range(PIECES)]


def kernel(
    n_row,
    n_col,
    tiles,
    col_ids,
    row_ids,
    x_own,
    xw_own,
    y_own,
    yw_own,
    start,
    row_out,
    col_out,
    x_all,
    xw_all,
    y_all,
    x_reduced,
    x_kept,
    y_reduced,
    y_kept,
    x_norm,
    score_a,
    score_b,
    peak_a,
    peak_b,
    slots,
    col_part,
    col_recv,
    col_send,
    bias_all,
    row_part,
    row_recv,
    row_total,
    x_ssem,
    x_rsem,
    w_ssem,
    w_rsem,
    y_ssem,
    y_rsem,
    c_ssem,
    c_rsem,
    b_ssem,
    b_rsem,
    r_ssem,
    r_rsem,
):
    me_row = lax.axis_index("row")
    me_col = lax.axis_index("col")
    n_slot = slots.shape[0]
    row_blocks = x_all.shape[0]
    own_blocks = x_own.shape[0]

    def along_row(d):
        return lax.rem(me_row + d, n_row)

    def along_col(d):
        return lax.rem(me_col + d, n_col)

    barrier = pltpu.get_barrier_semaphore()

    def greet(d, carry):
        pl.semaphore_signal(
            barrier, inc=1, device_id={"row": along_row(d)}, device_id_type=MESH
        )
        return carry

    lax.fori_loop(1, n_row, greet, 0)
    for d in range(1, n_col):
        pl.semaphore_signal(
            barrier, inc=1, device_id={"col": along_col(d)}, device_id_type=MESH
        )
    pl.semaphore_wait(barrier, n_row - 1 + n_col - 1)

    def x_copy(target, owner):
        return pltpu.make_async_remote_copy(
            src_ref=x_own,
            dst_ref=x_all.at[pl.ds(owner * own_blocks, own_blocks)],
            send_sem=x_ssem.at[target],
            recv_sem=x_rsem.at[owner],
            device_id={"col": target},
            device_id_type=MESH,
        )

    def w_copy(target, owner):
        return pltpu.make_async_remote_copy(
            src_ref=xw_own,
            dst_ref=xw_all.at[pl.ds(owner * own_blocks, own_blocks)],
            send_sem=w_ssem.at[target],
            recv_sem=w_rsem.at[owner],
            device_id={"col": target},
            device_id_type=MESH,
        )

    def y_copy(target, owner):
        return pltpu.make_async_remote_copy(
            src_ref=y_own,
            dst_ref=y_all.at[owner],
            send_sem=y_ssem.at[target],
            recv_sem=y_rsem.at[owner],
            device_id={"row": target},
            device_id_type=MESH,
        )

    def c_copy(it, target, owner):
        return pltpu.make_async_remote_copy(
            src_ref=col_part.at[it, target],
            dst_ref=col_recv.at[it, owner],
            send_sem=c_ssem.at[it, target],
            recv_sem=c_rsem.at[it, owner],
            device_id={"row": target},
            device_id_type=MESH,
        )

    def b_copy(it, target, owner):
        return pltpu.make_async_remote_copy(
            src_ref=col_send.at[it],
            dst_ref=bias_all.at[it, owner],
            send_sem=b_ssem.at[it, target],
            recv_sem=b_rsem.at[it, owner],
            device_id={"row": target},
            device_id_type=MESH,
        )

    def r_copy(it, target, owner):
        return pltpu.make_async_remote_copy(
            src_ref=row_part.at[it],
            dst_ref=row_recv.at[it, owner],
            send_sem=r_ssem.at[it, target],
            recv_sem=r_rsem.at[it, owner],
            device_id={"col": target},
            device_id_type=MESH,
        )

    for d in range(1, n_col):
        x_copy(along_col(d), me_col).start()
        w_copy(along_col(d), me_col).start()

    def y_start(d, carry):
        y_copy(along_row(d), me_row).start()
        return carry

    lax.fori_loop(1, n_row, y_start, 0)

    place_points(y_own[...], y_reduced, y_kept, me_row)
    y_norm = jnp.sum(y_own[...] * y_own[...], axis=0, keepdims=True)
    for d in range(own_blocks):
        x_all[me_col * own_blocks + d] = x_own[d]
        xw_all[me_col * own_blocks + d] = xw_own[d]
    for d in range(1, n_col):
        x_copy(me_col, along_col(d)).wait_recv()
        w_copy(me_col, along_col(d)).wait_recv()

    def x_block(b, carry):
        points = x_all[b]
        place_points(points * SCALE, x_reduced, x_kept, b)
        norm = cut(jnp.sum(points * points, axis=0, keepdims=True))
        for k in range(PIECES):
            x_norm[b, k : k + 1, :] = norm[k]
        bias = xw_all[b] + (start[b] - x_norm[b]) * (1.0 / epsilon)
        place_bias(bias * LOG2E, x_reduced, b)
        return carry

    lax.fori_loop(0, row_blocks, x_block, 0)

    def y_block(d, carry):
        owner = along_row(d)
        y_copy(me_row, owner).wait_recv()
        place_points(y_all[owner], y_reduced, y_kept, owner)
        return carry

    lax.fori_loop(1, n_row, y_block, 0)

    def visit(reduced, kept, by_column):
        def begin(slot, score, peak):
            tile = tiles[lax.rem(slot, n_slot)]
            row = lax.div(tile, n_row)
            col = lax.rem(tile, n_row)
            left, right = (row, col) if by_column else (col, row)
            value = lax.dot_general(
                reduced[left],
                kept[right],
                (((0,), (0,)), ((), ())),
                preferred_element_type=jnp.float32,
            )
            score[...] = value
            peak[...] = jnp.max(value, axis=0, keepdims=True)

        def finish(slot, score, peak):
            top = peak[...]
            total = jnp.sum(jnp.exp2(score[...] - top), axis=0, keepdims=True)
            slots[pl.ds(slot, 1), :] = top + jnp.log2(total)

        begin(0, score_a, peak_a)

        def pair(i, carry):
            begin(2 * i + 1, score_b, peak_b)
            finish(2 * i, score_a, peak_a)
            begin(2 * i + 2, score_a, peak_a)
            finish(2 * i + 1, score_b, peak_b)
            return carry

        lax.fori_loop(0, n_slot // 2, pair, 0)

    def fold(ids, block):
        return cut(lse(jnp.where(ids[...] == block, slots[...], lowest)))

    def iteration(it, carry):
        visit(x_reduced, y_kept, True)

        def col_fold(c, inner):
            line = fold(col_ids, c)
            for k in range(PIECES):
                col_part[it, c, k : k + 1, :] = line[k]
            return inner

        lax.fori_loop(0, n_row, col_fold, 0)

        def c_start(d, inner):
            c_copy(it, along_row(d), me_row).start()
            return inner

        lax.fori_loop(1, n_row, c_start, 0)
        col_recv[it, me_row] = col_part[it, me_row]

        def c_wait(d, inner):
            c_copy(it, me_row, along_row(d)).wait_recv()
            return inner

        lax.fori_loop(1, n_row, c_wait, 0)
        total = lse(col_recv[it])[0]
        bias = yw_own[...] * LOG2E - total
        norm = cut(y_norm)
        for k in range(PIECES):
            col_send[it, k : k + 1, :] = bias[k : k + 1]
            dual = norm[k] - (epsilon * LN2) * total[k : k + 1]
            col_send[it, PIECES + k : PIECES + k + 1, :] = dual

        def b_start(d, inner):
            b_copy(it, along_row(d), me_row).start()
            return inner

        lax.fori_loop(1, n_row, b_start, 0)
        bias_all[it, me_row] = col_send[it]

        place_bias(bias_all[it, me_row], y_reduced, me_row)

        def b_wait(d, inner):
            owner = along_row(d)
            b_copy(it, me_row, owner).wait_recv()
            place_bias(bias_all[it, owner], y_reduced, owner)
            return inner

        lax.fori_loop(1, n_row, b_wait, 0)

        visit(y_reduced, x_kept, False)

        def row_fold(b, inner):
            line = fold(row_ids, b)
            for k in range(PIECES):
                row_part[it, b, k : k + 1, :] = line[k]
            return inner

        lax.fori_loop(0, row_blocks, row_fold, 0)
        for d in range(1, n_col):
            r_copy(it, along_col(d), me_col).start()
        row_recv[it, me_col] = row_part[it]
        for d in range(1, n_col):
            r_copy(it, me_col, along_col(d)).wait_recv()
        row_total[...] = lse(row_recv[it])[0]

        def row_bias(b, inner):
            place_bias(xw_all[b] * LOG2E - row_total[b], x_reduced, b)
            return inner

        lax.fori_loop(0, row_blocks, row_bias, 0)
        return carry

    lax.fori_loop(0, ITERS, iteration, 0)

    row_out[...] = x_norm[...] - (epsilon * LN2) * row_total[...]

    def result(c, carry):
        col_out[c] = bias_all[ITERS - 1, c, PIECES:, :]
        return carry

    lax.fori_loop(0, n_row, result, 0)

    for d in range(1, n_col):
        x_copy(along_col(d), me_col).wait_send()
        w_copy(along_col(d), me_col).wait_send()
        for it in range(ITERS):
            r_copy(it, along_col(d), me_col).wait_send()

    def sent(d, carry):
        y_copy(along_row(d), me_row).wait_send()
        for it in range(ITERS):
            c_copy(it, along_row(d), me_row).wait_send()
            b_copy(it, along_row(d), me_row).wait_send()
        return carry

    lax.fori_loop(1, n_row, sent, 0)


def per_device(
    n_row,
    n_col,
    samples,
    sample_logw,
    references,
    reference_logw,
    dual_start,
    kept_tiles,
    tile_counts,
):
    own_blocks = samples.shape[0] // TILE
    row_blocks = own_blocks * n_col
    dim = samples.shape[1]
    n_slot = kept_tiles.shape[2]
    tiles = kept_tiles[0, 0]
    used = jnp.arange(n_slot, dtype=jnp.int32) < tile_counts[0, 0]
    col_ids = jnp.where(used, tiles % n_row, -1)
    row_ids = jnp.where(used, tiles // n_row, -1)
    x_own = samples.reshape(own_blocks, TILE, dim).transpose(0, 2, 1)
    f32 = jnp.float32
    bf16 = jnp.bfloat16
    dma = pltpu.SemaphoreType.DMA
    vmem = pltpu.VMEM
    row_dual, col_dual = pl.pallas_call(
        functools.partial(kernel, n_row, n_col),
        out_shape=(
            jax.ShapeDtypeStruct((row_blocks, PIECES, LANES), f32),
            jax.ShapeDtypeStruct((n_row, PIECES, LANES), f32),
        ),
        in_specs=[pl.BlockSpec(memory_space=pltpu.SMEM)]
        + [pl.BlockSpec(memory_space=pltpu.VMEM)] * 7,
        out_specs=(pl.BlockSpec(memory_space=pltpu.VMEM),) * 2,
        scratch_shapes=[
            vmem((row_blocks, dim, TILE), f32),
            vmem((row_blocks, PIECES, LANES), f32),
            vmem((n_row, dim, TILE), f32),
            vmem((row_blocks, DEPTH, TILE), bf16),
            vmem((row_blocks, DEPTH, TILE), bf16),
            vmem((n_row, DEPTH, TILE), bf16),
            vmem((n_row, DEPTH, TILE), bf16),
            vmem((row_blocks, PIECES, LANES), f32),
            vmem((TILE, TILE), f32),
            vmem((TILE, TILE), f32),
            vmem((1, TILE), f32),
            vmem((1, TILE), f32),
            vmem((n_slot, TILE), f32),
            vmem((ITERS, n_row, PIECES, LANES), f32),
            vmem((ITERS, n_row, PIECES, LANES), f32),
            vmem((ITERS, 2 * PIECES, LANES), f32),
            vmem((ITERS, n_row, 2 * PIECES, LANES), f32),
            vmem((ITERS, row_blocks, PIECES, LANES), f32),
            vmem((ITERS, n_col, row_blocks, PIECES, LANES), f32),
            vmem((row_blocks, PIECES, LANES), f32),
            dma((n_col,)),
            dma((n_col,)),
            dma((n_col,)),
            dma((n_col,)),
            dma((n_row,)),
            dma((n_row,)),
            dma((ITERS, n_row)),
            dma((ITERS, n_row)),
            dma((ITERS, n_row)),
            dma((ITERS, n_row)),
            dma((ITERS, n_col)),
            dma((ITERS, n_col)),
        ],
        compiler_params=pltpu.CompilerParams(
            collective_id=0, has_side_effects=True, vmem_limit_bytes=48 * 2**20
        ),
        name="sinkhorn",
    )(
        tiles,
        jnp.broadcast_to(col_ids[:, None], (n_slot, TILE)),
        jnp.broadcast_to(row_ids[:, None], (n_slot, TILE)),
        x_own,
        sample_logw.reshape(own_blocks, PIECES, LANES),
        references.T,
        reference_logw.reshape(PIECES, LANES),
        dual_start.reshape(row_blocks, PIECES, LANES),
    )
    return row_dual.reshape(1, -1), col_dual.reshape(1, -1)


def solution(mesh):
    n_row, n_col = mesh.shape["row"], mesh.shape["col"]
    both = ("row", "col")
    in_specs = (
        P(both, None),
        P(both),
        P(both, None),
        P(both),
        P("row", None),
        P("row", "col", None),
        P("row", "col"),
    )
    out_specs = (P("row", None), P("col", None))
    return jax.shard_map(
        functools.partial(per_device, n_row, n_col),
        mesh=mesh,
        in_specs=in_specs,
        out_specs=out_specs,
        check_vma=False,
    )
```

time: 991 us -> 166 us (0.17); the launches traced: 975 us -> 166 us
  matrix products: 228 us -> 0 us
  blocking collectives: 218 us -> 0 us
  local copies, waits for them, and re-layouts: 190 us -> 2.96 us
  Pallas kernels: 0 us -> 162 us
  loops' own time: 134 us -> 0 us
  waiting for transfers between devices: 122 us -> 0 us
  other arithmetic: 46.9 us -> 0.01 us
  starting transfers between devices: 21.1 us -> 0 us
  between operations: 16.5 us -> 1.32 us
    dot_general x102 -> x0, matrix products: 228 us -> none  [tile_cost(): jnp.dot(row_points, col_points.T, precision=lax.Precision.HIGHEST, prefer...]
    all_gather x19 -> x0, blocking collectives: 173 us -> none  [the longest x18 161 us: combined_by_axis(): pieces = jax.tree.map(lambda part: lax.all_gather(part, axis), shard)]
    pallas_call x0 -> x1, Pallas kernels: none -> 162 us  [per_device(): pl.pallas_call(functools.partial(kernel, n_row, n_col), out_shape=(jax.Sh...]
    dynamic_slice x612 -> x0, local copies, waits for them, and re-layouts: 153 us -> none  [the longest x102 63 us: locate(): high_tiles[jnp.clip(position - low_count, 0, slots - 1)]]
    another operation x6 -> x0, loops' own time: 134 us -> none  [the longest x3 66.8 us: per_device(): row_peaks, row_sums = lax.fori_loop(0, work, row_visit, start_state)]
    all_gather x1 -> x0, waiting for transfers between devices: 101 us -> none  [side_by_side(): lax.all_gather(both, axis, axis=dim, tiled=True)]
    all_to_all x2 -> x0, blocking collectives: 45 us -> none  [from_everyone(): lax.all_to_all(jnp.broadcast_to(shard[None], (devices, *shard.shape)), ax...]
    dynamic_update_slice x102 -> x0, local copies, waits for them, and re-layouts: 26.3 us -> none  [the longest x51 13.1 us: row_visit(): lax.dynamic_update_slice(carry[0], merged[0][None], (source, row_start))]
  transfers between devices with their start and end apart: 15 -> 0, of which waited for: 11 -> 0; matrix products, arithmetic and copies ran while one was open for 1% -> 0% of each run, Pallas kernels for 0% -> 0%
where the time goes in v1:
time: 166 us
  Pallas kernels  162 us (98%)
  local copies, waits for them, and re-layouts  2.96 us (2%)
    pallas_call x1, Pallas kernels, per_device(): pl.pallas_call(functools.partial(kernel, n_row, n_col), out_shape=(jax.Sh...  162 us

profile of v1, /device:TPU:1, one launch (start us, length us, event | category | flops | bytes accessed | tf_op | source)
XLA Modules:
  0.0 165.9 jit_solution(6401860774634975263)
XLA Ops:
  1.3 0.0 copy-start.4
  1.3 0.0 copy-start.5
  1.3 0.6 copy-done.4
  1.9 0.1 broadcast_in_dim.19.row_ids
  2.0 0.1 broadcast_in_dim.18.col_ids
  2.1 0.1 copy-done.5
  2.2 0.0 copy-start
  2.2 0.0 copy-start.1
  2.2 0.0 copy-start.2
  2.2 0.0 copy-start.3
  2.2 0.8 copy-done
  3.0 0.0 copy-done.1
  3.0 0.0 copy-done.2
  3.0 0.0 copy-done.3
  3.0 161.7 %sinkhorn.1 = (f32[8,4,128]{2,1,0:T(4,128)S(1)}, f32[32,4,128]{2,1,0:T(4,128)S(1)}) custom-call(s32[32]{0:T(128)S(1)} %bitcast.29, s32[32,512]{1,0:T(8,128)S(1)} %broadcast_in_dim.18.col_ids, s32[32,512]{1,0:T(8,128)S(1)} %broadcast_in_dim.19.row_ids, f32[2,32,512]{2,1,0:T(8,128)S(1)} %bitcast.22, f32[2,4,128]{2,1,0:T(4,128)S(1)} %bitcast.27, ...), custom_call_target="tpu_custom_call" | custom-call | tf_op jit(solution)/shard_map/sinkhorn/pallas_call | solution.py:394
  164.7 0.6 copy.16
  165.3 0.6 copy.17
  (2 shorter events, 0.0 us)
Async XLA Ops:
  1.3 0.7 copy-start.4
  1.3 0.9 copy-start.5
  2.2 0.8 copy-start
  2.2 0.8 copy-start.1
  2.2 0.8 copy-start.2
  2.2 0.8 copy-start.3

commit v2 on v1

--- a/solution.py
+++ b/solution.py
@@ -13,6 +13,10 @@
 PIECES = TILE // LANES
 DEPTH = 128
 BIAS = 16
+SUB = 8
+CHUNK = 64
+AT_ONCE = 8
+NX, NZ, NY = 4, 2, 4
 MESH = pl.DeviceIdType.MESH
 
 lowest = -1e30
@@ -33,13 +37,17 @@
     return high, low
 
 
-def place_points(points, reduced, kept, slot):
+def place_points(points, reduced, kept, slot, at, dim):
     high, low = halves(points)
-    dim = points.shape[0]
-    top = BIAS + 3 * dim
+    size = points.shape[0]
     for ref, order in ((reduced, (high, high, low)), (kept, (high, low, high))):
         for k, part in enumerate(order):
-            ref[slot, BIAS + k * dim : BIAS + (k + 1) * dim, :] = part
+            ref[slot, pl.ds(BIAS + k * dim + at, size), :] = part
+
+
+def fill(reduced, kept, slot, dim):
+    top = BIAS + 3 * dim
+    for ref in (reduced, kept):
         ref[slot, top:, :] = jnp.zeros((DEPTH - top, TILE), jnp.bfloat16)
     kept[slot, :BIAS, :] = jnp.ones((BIAS, TILE), jnp.bfloat16)
 
@@ -85,15 +93,12 @@
     y_reduced,
     y_kept,
     x_norm,
-    score_a,
-    score_b,
-    peak_a,
-    peak_b,
     slots,
     col_part,
     col_recv,
     col_send,
     bias_all,
+    dual_send,
     row_part,
     row_recv,
     row_total,
@@ -107,6 +112,8 @@
     c_rsem,
     b_ssem,
     b_rsem,
+    g_ssem,
+    g_rsem,
     r_ssem,
     r_rsem,
 ):
@@ -135,13 +142,24 @@
         pl.semaphore_signal(
             barrier, inc=1, device_id={"col": along_col(d)}, device_id_type=MESH
         )
+
+    def fill_y(c, carry):
+        fill(y_reduced, y_kept, c, y_own.shape[0])
+        return carry
+
+    def fill_x(b, carry):
+        fill(x_reduced, x_kept, b, y_own.shape[0])
+        return carry
+
+    lax.fori_loop(0, n_row, fill_y, 0)
+    lax.fori_loop(0, row_blocks, fill_x, 0)
     pl.semaphore_wait(barrier, n_row - 1 + n_col - 1)
 
-    def x_copy(target, owner):
-        return pltpu.make_async_remote_copy(
-            src_ref=x_own,
+    def x_copy(target, owner, turn, source):
+        return pltpu.make_async_remote_copy(
+            src_ref=source,
             dst_ref=x_all.at[pl.ds(owner * own_blocks, own_blocks)],
-            send_sem=x_ssem.at[target],
+            send_sem=x_ssem.at[turn],
             recv_sem=x_rsem.at[owner],
             device_id={"col": target},
             device_id_type=MESH,
@@ -157,12 +175,13 @@
             device_id_type=MESH,
         )
 
-    def y_copy(target, owner):
-        return pltpu.make_async_remote_copy(
-            src_ref=y_own,
-            dst_ref=y_all.at[owner],
-            send_sem=y_ssem.at[target],
-            recv_sem=y_rsem.at[owner],
+    def y_copy(target, owner, first, count, source=None):
+        rows = pl.ds(first * SUB, count * SUB)
+        return pltpu.make_async_remote_copy(
+            src_ref=y_all.at[owner, rows] if source is None else source.at[rows],
+            dst_ref=y_all.at[owner, rows],
+            send_sem=y_ssem,
+            recv_sem=y_rsem.at[owner, first],
             device_id={"row": target},
             device_id_type=MESH,
         )
@@ -187,6 +206,16 @@
             device_id_type=MESH,
         )
 
+    def g_copy(target, owner):
+        return pltpu.make_async_remote_copy(
+            src_ref=dual_send,
+            dst_ref=col_out.at[owner],
+            send_sem=g_ssem.at[target],
+            recv_sem=g_rsem.at[owner],
+            device_id={"row": target},
+            device_id_type=MESH,
+        )
+
     def r_copy(it, target, owner):
         return pltpu.make_async_remote_copy(
             src_ref=row_part.at[it],
@@ -197,28 +226,109 @@
             device_id_type=MESH,
         )
 
+    dim = y_own.shape[0]
+    groups = dim // SUB
+    half = groups // 2
+    at_x = lax.rem(me_row, NX)
+    at_z = lax.rem(lax.div(me_row, NX), NZ)
+    at_y = lax.div(me_row, NX * NZ)
+
+    def shifted(axis, shift, other, z):
+        steps = (shift, other) if axis == 0 else (other, shift)
+        return (
+            lax.rem(at_y + steps[1], NY) * (NX * NZ)
+            + lax.rem(at_z + z, NZ) * NX
+            + lax.rem(at_x + steps[0], NX)
+        )
+
+    def ring(axis, step):
+        return shifted(axis, step, 0, 0)
+
+    forward, back = 1, NX - 1
+
+    def send_half(axis, part, owner, source=None):
+        for step in (forward, back):
+            y_copy(ring(axis, step), owner, part * half, half, source).start()
+
+    def relay(axis, part, owner, step):
+        y_copy(me_row, owner, part * half, half).wait_recv()
+        piece = part * half + (0 if step == forward else half // 2)
+        y_copy(ring(axis, step), owner, piece, half // 2).start()
+
+    def arrive(part, owner):
+        for piece in range(2):
+            y_copy(me_row, owner, part * half + piece * (half // 2), half // 2).wait_recv()
+
+    def place_y(part, owner):
+        at = part * half * SUB
+        points = y_all[owner, at : at + half * SUB, :]
+        place_points(points, y_reduced, y_kept, owner, at, dim)
+
+    partner = shifted(0, 0, 0, 1)
+    y_copy(partner, me_row, 0, groups, y_own).start()
+    for part in range(2):
+        send_half(part, part, me_row, y_own)
+    beside = me_col + 1 - 2 * lax.rem(me_col, 2)
+    across = me_col + 2 - 4 * lax.rem(lax.div(me_col, 2), 2)
+    if n_col > 1:
+        x_copy(beside, me_col, 0, x_own).start()
+    if n_col > 2:
+        x_copy(across, me_col, 1, x_own).start()
     for d in range(1, n_col):
-        x_copy(along_col(d), me_col).start()
         w_copy(along_col(d), me_col).start()
 
-    def y_start(d, carry):
-        y_copy(along_row(d), me_row).start()
-        return carry
-
-    lax.fori_loop(1, n_row, y_start, 0)
-
-    place_points(y_own[...], y_reduced, y_kept, me_row)
     y_norm = jnp.sum(y_own[...] * y_own[...], axis=0, keepdims=True)
+    y_all[me_row] = y_own[...]
     for d in range(own_blocks):
         x_all[me_col * own_blocks + d] = x_own[d]
         xw_all[me_col * own_blocks + d] = xw_own[d]
+
+    y_copy(me_row, partner, 0, groups).wait_recv()
+    for part in range(2):
+        send_half(part, part, partner)
+    for z in range(NZ):
+        for part in range(2):
+            for step in (forward, back):
+                relay(part, part, shifted(part, NX - step, 0, z), step)
+    for part in range(2):
+        for z in range(NZ):
+            owner = shifted(part, 0, 0, z)
+            send_half(1 - part, part, owner, y_own if z == 0 else None)
+            for shift in (forward, back):
+                send_half(1 - part, part, shifted(part, shift, 0, z))
+    for part in range(2):
+        for z in range(NZ):
+            owner = shifted(part, 2, 0, z)
+            arrive(part, owner)
+            send_half(1 - part, part, owner)
+    if n_col > 2:
+        x_copy(me_col, across, 0, x_own).wait_recv()
+        relayed = x_all.at[pl.ds(across * own_blocks, own_blocks)]
+        x_copy(beside, across, 2, relayed).start()
+    for part in range(2):
+        for shift in range(NX):
+            for z in range(NZ):
+                place_y(part, shifted(part, shift, 0, z))
+
+    for shift in (0, 1, 3, 2):
+        for z in range(NZ):
+            for part in range(2):
+                for step in (forward, back):
+                    owner = shifted(part, shift, NY - step, z)
+                    relay(1 - part, part, owner, step)
+                    place_y(part, owner)
+
+    if n_col > 1:
+        x_copy(me_col, beside, 0, x_own).wait_recv()
+    if n_col > 2:
+        last = across + 1 - 2 * lax.rem(across, 2)
+        x_copy(me_col, last, 0, x_own).wait_recv()
     for d in range(1, n_col):
-        x_copy(me_col, along_col(d)).wait_recv()
         w_copy(me_col, along_col(d)).wait_recv()
 
     def x_block(b, carry):
         points = x_all[b]
-        place_points(points * SCALE, x_reduced, x_kept, b)
+        place_points(points * SCALE, x_reduced, x_kept, b, 0, dim)
         norm = cut(jnp.sum(points * points, axis=0, keepdims=True))
         for k in range(PIECES):
             x_norm[b, k : k + 1, :] = norm[k]
@@ -228,44 +338,43 @@
 
     lax.fori_loop(0, row_blocks, x_block, 0)
 
-    def y_block(d, carry):
-        owner = along_row(d)
-        y_copy(me_row, owner).wait_recv()
-        place_points(y_all[owner], y_reduced, y_kept, owner)
-        return carry
-
-    lax.fori_loop(1, n_row, y_block, 0)
+    for shift in (0, 1, 3, 2):
+        for z in range(NZ):
+            for part in range(2):
+                owner = shifted(part, shift, 2, z)
+                arrive(part, owner)
+                place_y(part, owner)
 
     def visit(reduced, kept, by_column):
-        def begin(slot, score, peak):
-            tile = tiles[lax.rem(slot, n_slot)]
+        def one(slot):
+            tile = tiles[slot]
             row = lax.div(tile, n_row)
             col = lax.rem(tile, n_row)
             left, right = (row, col) if by_column else (col, row)
-            value = lax.dot_general(
+            score = lax.dot_general(
                 reduced[left],
                 kept[right],
                 (((0,), (0,)), ((), ())),
                 preferred_element_type=jnp.float32,
             )
-            score[...] = value
-            peak[...] = jnp.max(value, axis=0, keepdims=True)
-
-        def finish(slot, score, peak):
-            top = peak[...]
-            total = jnp.sum(jnp.exp2(score[...] - top), axis=0, keepdims=True)
-            slots[pl.ds(slot, 1), :] = top + jnp.log2(total)
-
-        begin(0, score_a, peak_a)
-
-        def pair(i, carry):
-            begin(2 * i + 1, score_b, peak_b)
-            finish(2 * i, score_a, peak_a)
-            begin(2 * i + 2, score_a, peak_a)
-            finish(2 * i + 1, score_b, peak_b)
+            peaks, sums = [], []
+            for at in range(0, TILE, CHUNK):
+                part = score[at : at + CHUNK].reshape(CHUNK // SUB, SUB, TILE)
+                peak = jnp.max(part, axis=0)
+                peaks.append(peak)
+                sums.append(jnp.sum(jnp.exp2(part - peak[None]), axis=0))
+            top = functools.reduce(jnp.maximum, peaks)
+            total = sum(a * jnp.exp2(b - top) for a, b in zip(sums, peaks))
+            highest = jnp.max(top, axis=0, keepdims=True)
+            total = jnp.sum(total * jnp.exp2(top - highest), axis=0, keepdims=True)
+            slots[pl.ds(slot, 1), :] = highest + jnp.log2(total)
+
+        def several(i, carry):
+            for k in range(AT_ONCE):
+                one(i * AT_ONCE + k)
             return carry
 
-        lax.fori_loop(0, n_slot // 2, pair, 0)
+        lax.fori_loop(0, n_slot // AT_ONCE, several, 0)
 
     def fold(ids, block):
         return cut(lse(jnp.where(ids[...] == block, slots[...], lowest)))
@@ -279,7 +388,7 @@
                 col_part[it, c, k : k + 1, :] = line[k]
             return inner
 
-        lax.fori_loop(0, n_row, col_fold, 0)
+        lax.fori_loop(0, n_row, col_fold, 0, unroll=4)
 
         def c_start(d, inner):
             c_copy(it, along_row(d), me_row).start()
@@ -296,19 +405,26 @@
         total = lse(col_recv[it])[0]
         bias = yw_own[...] * LOG2E - total
         norm = cut(y_norm)
+        col_send[it] = bias
         for k in range(PIECES):
-            col_send[it, k : k + 1, :] = bias[k : k + 1]
-            dual = norm[k] - (epsilon * LN2) * total[k : k + 1]
-            col_send[it, PIECES + k : PIECES + k + 1, :] = dual
+            dual_send[k : k + 1, :] = norm[k] - (epsilon * LN2) * total[k : k + 1]
 
         def b_start(d, inner):
             b_copy(it, along_row(d), me_row).start()
             return inner
 
         lax.fori_loop(1, n_row, b_start, 0)
-        bias_all[it, me_row] = col_send[it]
-
-        place_bias(bias_all[it, me_row], y_reduced, me_row)
+
+        def g_start(d, inner):
+            g_copy(along_row(d), me_row).start()
+            return inner
+
+        @pl.when(it == ITERS - 1)
+        def _():
+            lax.fori_loop(1, n_row, g_start, 0)
+            col_out[me_row] = dual_send[...]
+
+        place_bias(bias, y_reduced, me_row)
 
         def b_wait(d, inner):
             owner = along_row(d)
@@ -326,7 +442,7 @@
                 row_part[it, b, k : k + 1, :] = line[k]
             return inner
 
-        lax.fori_loop(0, row_blocks, row_fold, 0)
+        lax.fori_loop(0, row_blocks, row_fold, 0, unroll=4)
         for d in range(1, n_col):
             r_copy(it, along_col(d), me_col).start()
         row_recv[it, me_col] = row_part[it]
@@ -345,20 +461,30 @@
 
     row_out[...] = x_norm[...] - (epsilon * LN2) * row_total[...]
 
-    def result(c, carry):
-        col_out[c] = bias_all[ITERS - 1, c, PIECES:, :]
-        return carry
-
-    lax.fori_loop(0, n_row, result, 0)
+    def result(d, carry):
+        g_copy(me_row, along_row(d)).wait_recv()
+        return carry
+
+    lax.fori_loop(1, n_row, result, 0)
 
     for d in range(1, n_col):
-        x_copy(along_col(d), me_col).wait_send()
         w_copy(along_col(d), me_col).wait_send()
         for it in range(ITERS):
             r_copy(it, along_col(d), me_col).wait_send()
 
+    for turn in range(min(n_col - 1, 3)):
+        x_copy(beside, me_col, turn, x_own).wait_send()
+    pltpu.make_async_remote_copy(
+        src_ref=y_all.at[pl.ds(0, n_row - 1)],
+        dst_ref=y_all.at[pl.ds(0, n_row - 1)],
+        send_sem=y_ssem,
+        recv_sem=y_rsem.at[0, 0],
+        device_id={"row": partner},
+        device_id_type=MESH,
+    ).wait_send()
+
     def sent(d, carry):
-        y_copy(along_row(d), me_row).wait_send()
+        g_copy(along_row(d), me_row).wait_send()
         for it in range(ITERS):
             c_copy(it, along_row(d), me_row).wait_send()
             b_copy(it, along_row(d), me_row).wait_send()
@@ -409,28 +535,27 @@
             vmem((n_row, DEPTH, TILE), bf16),
             vmem((n_row, DEPTH, TILE), bf16),
             vmem((row_blocks, PIECES, LANES), f32),
-            vmem((TILE, TILE), f32),
-            vmem((TILE, TILE), f32),
-            vmem((1, TILE), f32),
-            vmem((1, TILE), f32),
             vmem((n_slot, TILE), f32),
             vmem((ITERS, n_row, PIECES, LANES), f32),
             vmem((ITERS, n_row, PIECES, LANES), f32),
-            vmem((ITERS, 2 * PIECES, LANES), f32),
-            vmem((ITERS, n_row, 2 * PIECES, LANES), f32),
+            vmem((ITERS, PIECES, LANES), f32),
+            vmem((ITERS, n_row, PIECES, LANES), f32),
+            vmem((PIECES, LANES), f32),
             vmem((ITERS, row_blocks, PIECES, LANES), f32),
             vmem((ITERS, n_col, row_blocks, PIECES, LANES), f32),
             vmem((row_blocks, PIECES, LANES), f32),
+            dma((3,)),
             dma((n_col,)),
             dma((n_col,)),
             dma((n_col,)),
-            dma((n_col,)),
-            dma((n_row,)),
-            dma((n_row,)),
+            dma,
+            dma((n_row, dim // SUB)),
             dma((ITERS, n_row)),
             dma((ITERS, n_row)),
             dma((ITERS, n_row)),
             dma((ITERS, n_row)),
+            dma((n_row,)),
+            dma((n_row,)),
             dma((ITERS, n_col)),
             dma((ITERS, n_col)),
         ],

time: 166 us -> 130 us (0.78)
  Pallas kernels: 162 us -> 126 us
    pallas_call x1, Pallas kernels: 162 us -> 126 us  [per_device(): pl.pallas_call(functools.partial(kernel, n_row, n_col), out_shape=(jax.Sh...]
where the time goes in v2:
time: 130 us
  Pallas kernels  126 us (97%)
  local copies, waits for them, and re-layouts  2.96 us (2%)
  between operations  1.32 us (1%)
    pallas_call x1, Pallas kernels, per_device(): pl.pallas_call(functools.partial(kernel, n_row, n_col), out_shape=(jax.Sh...  126 us
    unnamed x14, local copies, waits for them, and re-layouts  2.81 us

profile of v2, /device:TPU:1, one launch (start us, length us, event | category | flops | bytes accessed | tf_op | source)
XLA Modules:
  0.0 130.0 jit_solution(12450206475020131820)
XLA Ops:
  1.3 0.0 copy-start.4
  1.3 0.0 copy-start.5
  1.3 0.6 copy-done.4
  1.9 0.1 broadcast_in_dim.19.row_ids
  2.0 0.1 broadcast_in_dim.18.col_ids
  2.1 0.1 copy-done.5
  2.2 0.0 copy-start
  2.2 0.0 copy-start.1
  2.2 0.0 copy-start.2
  2.2 0.0 copy-start.3
  2.2 0.8 copy-done
  3.0 0.0 copy-done.1
  3.0 0.0 copy-done.2
  3.0 0.0 copy-done.3
  3.0 125.7 %sinkhorn.1 = (f32[8,4,128]{2,1,0:T(4,128)S(1)}, f32[32,4,128]{2,1,0:T(4,128)S(1)}) custom-call(s32[32]{0:T(128)S(1)} %bitcast.29, s32[32,512]{1,0:T(8,128)S(1)} %broadcast_in_dim.18.col_ids, s32[32,512]{1,0:T(8,128)S(1)} %broadcast_in_dim.19.row_ids, f32[2,32,512]{2,1,0:T(8,128)S(1)} %bitcast.22, f32[2,4,128]{2,1,0:T(4,128)S(1)} %bitcast.27, ...), custom_call_target="tpu_custom_call" | custom-call | tf_op jit(solution)/shard_map/sinkhorn/pallas_call | solution.py:520
  128.7 0.6 copy.16
  129.3 0.6 copy.17
  (2 shorter events, 0.0 us)
Async XLA Ops:
  1.3 0.7 copy-start.4
  1.3 0.9 copy-start.5
  2.2 0.8 copy-start
  2.2 0.8 copy-start.1
  2.2 0.8 copy-start.2
  2.2 0.8 copy-start.3
